TPU v7x, 128 devices: a whole 4x4x4 slice. The times are simulated.
128 devices in a mesh: sensor: 16 (over y, z_lo, core), channel: 4 (over x), tm: 2 (over z_hi).
Axes of the slice: x: 4, y: 4, z: 4 (z_hi: 2, z_lo: 2; z = z_hi * 2 + z_lo), core: 2. Of those that a mesh axis runs over, the one named last changes fastest.
Arguments:
- tensor: float32 [12288, 128, 512], P('sensor', 'tm', 'channel'), may hold values from -6 to 6
- core: float32 [64, 64, 32], replicated, may hold values from -0.015625 to 0.015625
- sensor_factor: float32 [12288, 64], P('sensor'), may hold values from -6 to 6
- channel_factor: float32 [512, 64], P('channel'), may hold values from -6 to 6
- time_factor: float32 [128, 32], P('tm'), may hold values from -6 to 6
- neighbour_ids: int32 [96, 4], P('sensor'), may hold values from 0 to 95
- edge_weights: int32 [96, 4, 128, 128], P('sensor'), may hold values from 0 to 3
Outputs:
- core_grad: float32 [64, 64, 32], replicated
- sensor_grad: float32 [12288, 64], P(('sensor', 'channel', 'tm'))
- channel_grad: float32 [512, 64], P('channel')
- time_grad: float32 [128, 32], P('tm')
All inputs are finite; a program needn't handle non-finite values.
Results may differ from a plain program's by a relative error of at most 0.0001.
Values sent between devices are 32-bit elements; how exact they have to be, the bound alone decides.
A program may use at most 192 MiB of HBM per device.

v0:
```python
import math
import jax
import jax.numpy as jnp
from jax import lax
from jax.sharding import PartitionSpec as P

lap_weight = 1.0 / 512.0
highest = lax.Precision.HIGHEST


def pulled_rows(whole_factor, neighbour_ids, weights_float, block):
    whole = whole_factor.reshape(-1, block, whole_factor.shape[-1])
    neighbours = whole[neighbour_ids]
    return jnp.einsum("bnic,bncd->bid", weights_float, neighbours, precision=highest)


def on_device(
    tensor, core, sensor_factor, channel_factor, time_factor, neighbour_ids, edge_weights
):
    sensor_rows, time_rows, chan_rows = tensor.shape
    rank_one, rank_two, rank_three = core.shape
    n_sensor = lax.axis_size("sensor")
    n_channel = lax.axis_size("channel")
    n_time = lax.axis_size("tm")
    total_sensors = sensor_rows * n_sensor
    total_time = time_rows * n_time
    total_chan = chan_rows * n_channel
    core_time = jnp.einsum("rst,kt->rks", core, time_factor, precision=highest)
    core_both = jnp.einsum("rks,js->rkj", core_time, channel_factor, precision=highest)
    core_chan = jnp.einsum("rst,js->rtj", core, channel_factor, precision=highest)
    flat_core = core_both.reshape(rank_one, time_rows * chan_rows)
    residual = jnp.dot(sensor_factor, flat_core, precision=highest) - tensor.reshape(
        sensor_rows, time_rows * chan_rows
    )
    folded = jnp.dot(sensor_factor.T, residual, precision=highest)
    fit_part = jnp.dot(residual, flat_core.T, precision=highest) / math.sqrt(
        total_time * total_chan
    )
    folded3 = folded.reshape(rank_one, time_rows, chan_rows)
    inner = jnp.einsum("rkj,js->rks", folded3, channel_factor, precision=highest)
    core_part = jnp.einsum("rks,kt->rst", inner, time_factor, precision=highest) / math.sqrt(
        total_sensors * total_time * total_chan
    )
    chan_part = jnp.einsum("rkj,rks->js", folded3, core_time, precision=highest) / math.sqrt(
        total_sensors * total_time
    )
    time_part = jnp.einsum("rkj,rtj->kt", folded3, core_chan, precision=highest) / math.sqrt(
        total_sensors * total_chan
    )
    groups = n_channel * n_time
    share_index = lax.axis_index("channel") * n_time + lax.axis_index("tm")
    share = sensor_rows // groups
    block = edge_weights.shape[-1]
    weights_float = edge_weights.astype(jnp.float32)
    degree = jnp.sum(weights_float, axis=(1, 3)).reshape(sensor_rows)
    reduced = lax.psum_scatter(fit_part, ("channel", "tm"), scatter_dimension=0, tiled=True)
    whole_rows = lax.all_gather(sensor_factor, "sensor", axis=0, tiled=True)
    pulled = pulled_rows(whole_rows, neighbour_ids, weights_float, block).reshape(
        sensor_rows, rank_one
    )
    graph_all = lap_weight * (degree[:, None] * sensor_factor - pulled)
    graph_share = lax.dynamic_slice_in_dim(graph_all, share_index * share, share, 0)
    sensor_grad = reduced + graph_share
    core_grad = lax.psum(core_part, ("sensor", "channel", "tm"))
    channel_grad = lax.psum(chan_part, ("sensor", "tm"))
    time_grad = lax.psum(time_part, ("sensor", "channel"))
    return (core_grad, sensor_grad, channel_grad, time_grad)


def solution(mesh):
    return jax.shard_map(
        on_device,
        mesh=mesh,
        in_specs=(
            P("sensor", "tm", "channel"),
            P(),
            P("sensor", None),
            P("channel", None),
            P("tm", None),
            P("sensor", None),
            P("sensor", None, None, None),
        ),
        out_specs=(P(), P(("sensor", "channel", "tm"), None), P("channel", None), P("tm", None)),
        check_vma=False,
    )
```

profile of v0, /device:TPU:0, one launch (start us, length us, event | category | flops | bytes accessed | tf_op | source)
XLA Modules:
  0.0 556.5 jit_solution(13374377818562630704)
XLA Ops:
  8.0 0.0 copy-start
  8.0 0.0 copy-start.6
  8.0 0.0 reduce-scatter.4.cloned.1.call-start
  8.1 24.9 %copy.27 = f32[768,64,128]{0,2,1:T(8,128)} copy(f32[768,64,128]{2,1,0:T(8,128)} %param.7) | data formatting | bytes 50331648 | tf_op args[0]
  33.0 0.0 copy-done
  33.0 0.0 copy-done.6
  33.0 0.0 copy-start.5
  33.0 1.8 fusion.32
  34.8 0.0 copy-done.5
  34.8 0.0 copy-start.1
  34.8 0.0 copy-start.3
  34.8 1.8 fusion.5
  36.7 0.0 copy-done.1
  36.7 0.0 copy-done.3
  36.7 26.3 %bitcast_subtract_fusion = f32[768,8192]{0,1:T(8,128)} fusion(f32[768,64,128]{0,2,1:T(8,128)} %copy.27, f32[768,64]{0,1:T(8,128)S(1)} %copy-done.3, f32[8,8,64,128]{3,2,1,0:T(8,128)S(1)} %bitcast.77), kind=kOutput, calls=%fused_computation.1 | convolution fusion | flops 4838129664 | bytes 52625408 | tf_op jit(solution)/shard_map/dot_general | solution.py:32
  63.0 0.0 copy-start.4
  63.0 20.9 %fusion.14 = f32[768,64]{0,1:T(8,128)S(1)} fusion(f32[768,8192]{0,1:T(8,128)} %bitcast_subtract_fusion, f32[8,8,64,128]{3,2,1,0:T(8,128)S(1)} %bitcast.78), kind=kOutput, calls=%fused_computation.18 | convolution fusion | flops 4831887360 | bytes 27459584 | tf_op jit(solution)/shard_map/dot_general | solution.py:36
  83.8 0.9 copy.34
  84.8 0.0 reduce-scatter.4.cloned.1.call-update
  84.8 0.0 all-gather.2.cloned.1.call-start
  84.8 0.5 all-gather.2.cloned.1.call-update
  85.4 0.0 all-reduce.2.cloned.1.call-start
  85.4 0.0 copy-done.4
  85.4 27.7 %convolution_bitcast_fusion = f32[8,8,64,128]{3,1,2,0:T(8,128)S(1)} fusion(f32[768,8192]{0,1:T(8,128)} %bitcast_subtract_fusion, f32[768,64]{0,1:T(8,128)S(1)} %copy-done.4), kind=kOutput, calls=%fused_computation.12 | convolution fusion | flops 4831838208 | bytes 27459584 | tf_op jit(solution)/shard_map/dot_general | solution.py:35
  113.1 0.4 copy.39
  113.5 1.9 fusion.28
  115.4 2.2 convolution_multiply_fusion
  117.6 0.0 all-reduce.2.cloned.1.call-update
  117.6 5.2 fusion.20
  122.9 0.0 copy-start.7
  122.9 1.9 fusion.26
  124.8 0.0 copy-done.7
  124.8 0.1 copy.28
  124.9 0.1 reshape.31
  125.0 1.6 convert_reduce_fusion
  126.6 129.7 %psum.22 = f32[128,64]{0,1:T(8,128)} all-reduce(f32[128,64]{0,1:T(8,128)S(1)} %fusion.20), channel_id=1, replica_groups=mesh['sensor'=16,'channel'=4,'tm'=2] {'sensor','tm'}, use_global_device_ids=true, to_apply=%region_3.0 | all-reduce | flops 8192 | bytes 65536 | tf_op jit(solution)/shard_map/psum | solution.py:65
  256.3 3.0 fusion.23
  259.3 276.5 %psum.23 = f32[64,32]{0,1:T(8,128)} all-reduce(f32[64,32]{0,1:T(8,128)S(1)} %fusion.23), channel_id=1, replica_groups=mesh['sensor'=16,'channel'=4,'tm'=2] {'sensor','channel'}, use_global_device_ids=true, to_apply=%region_4.0 | all-reduce | flops 2048 | bytes 16384 | tf_op jit(solution)/shard_map/psum | solution.py:66
  535.8 0.1 dynamic-slice
  535.9 0.0 reduce-scatter.4.cloned.1.call-done
  535.9 0.9 copy.35
  536.8 0.0 all-gather.2.cloned.1.call-done
  536.8 4.0 copy_bitcast_fusion
  540.8 0.0 copy-start.2
  540.8 2.6 gather_fusion
  543.4 0.0 copy-done.2
  543.4 1.8 fusion.11
  545.2 1.6 fusion.25
  546.8 0.0 all-reduce.2.cloned.1.call-done
  546.8 2.3 copy.54
  (3 shorter events, 0.0 us)
Async XLA Ops:
  8.0 25.0 %copy-start = (f32[64,64,32]{1,2,0:T(8,128)S(1)}, f32[64,64,32]{1,2,0:T(8,128)}, u32[]{:S(2)}) copy-start(f32[64,64,32]{1,2,0:T(8,128)} %param.8) | copy-start | bytes 1572868
  8.0 24.9 %copy-start.6 = (f32[64,32]{0,1:T(8,128)S(1)}, f32[64,32]{0,1:T(8,128)}, u32[]{:S(2)}) copy-start(f32[64,32]{0,1:T(8,128)} %param.11) | copy-start | bytes 24580
  8.0 527.9 %reduce-scatter.4.cloned.1.call-start = ((), (), s32[]{:S(2)}) async-start(), calls=%async_computation.3 | async-start | bytes 442368
  33.0 1.8 copy-start.5
  34.8 1.9 copy-start.1
  34.8 1.9 copy-start.3
  63.0 22.5 %copy-start.4 = (f32[768,64]{0,1:T(8,128)S(1)}, f32[768,64]{0,1:T(8,128)}, u32[]{:S(2)}) copy-start(f32[768,64]{0,1:T(8,128)} %param.9) | copy-start | bytes 589828
  84.8 452.0 %all-gather.2.cloned.1.call-start = ((), (), s32[]{:S(2)}) async-start(), calls=%async_computation.2 | async-start | bytes 3342336 | tf_op jit(solution)/shard_map/all_gather | solution.py:57
  85.4 461.4 %all-reduce.2.cloned.1.call-start = ((), (), s32[]{:S(2)}) async-start(), calls=%async_computation.1 | async-start | bytes 2097152 | tf_op jit(solution)/shard_map/psum | solution.py:64
  122.9 1.9 copy-start.7
  540.8 2.6 copy-start.2
Sparse Core Ops, SparseCore 0:
  84.9 73.7 reduce-scatter.3
  164.1 146.2 all-reduce.1
Sparse Core Ops, SparseCore 1:
  87.0 38.2 all-gather.1
where the time goes:
time: 557 us; the launch traced here: 556 us
  blocking collectives  406 us (73%)
  matrix products  94.5 us (17%)
  local copies, waits for them, and re-layouts  36.2 us (6%)
  between operations  15.7 us (3%)
    psum x1, blocking collectives, on_device(): time_grad = lax.psum(time_part, ('sensor', 'channel'))  277 us
    psum x1, blocking collectives, on_device(): channel_grad = lax.psum(chan_part, ('sensor', 'tm'))  130 us
    unnamed x21, local copies, waits for them, and re-layouts  29.4 us
    dot_general x1, matrix products, on_device(): folded = jnp.dot(sensor_factor.T, residual, precision=highest)  27.7 us
    dot_general x1, matrix products, on_device(): jnp.dot(sensor_factor, flat_core, precision=highest)  26.3 us
    dot_general x1, matrix products, on_device(): jnp.dot(residual, flat_core.T, precision=highest)  20.9 us
  transfers between devices with their start and end apart: 3, of which 0 were waited for; matrix products, arithmetic and copies ran while one was open for 10% of the time, Pallas kernels for 0%

commit v1 on v0

--- a/solution.py
+++ b/solution.py
@@ -63,7 +63,9 @@
     sensor_grad = reduced + graph_share
     core_grad = lax.psum(core_part, ("sensor", "channel", "tm"))
     channel_grad = lax.psum(chan_part, ("sensor", "tm"))
-    time_grad = lax.psum(time_part, ("sensor", "channel"))
+    time_grad = time_part
+    for s in ("channel", "sensor"):
+        time_grad = lax.psum(time_grad, s)
     return (core_grad, sensor_grad, channel_grad, time_grad)
 
 

time: 557 us -> 351 us (0.63)
  blocking collectives: 406 us -> 200 us
    psum x1 -> x2, blocking collectives: 277 us -> 69.8 us  [on_device(): time_grad = lax.psum(time_grad, s)]
  transfers between devices with their start and end apart: 3 -> 3, of which waited for: 0 -> 0; matrix products, arithmetic and copies ran while one was open for 10% -> 16% of each run, Pallas kernels for 0% -> 0%
where the time goes in v1:
time: 351 us; the launch traced here: 350 us
  blocking collectives  200 us (57%)
  matrix products  94.5 us (27%)
  local copies, waits for them, and re-layouts  36.2 us (10%)
  between operations  15.7 us (4%)
    psum x1, blocking collectives, on_device(): channel_grad = lax.psum(chan_part, ('sensor', 'tm'))  130 us
    psum x2, blocking collectives, on_device(): time_grad = lax.psum(time_grad, s)  69.8 us
    unnamed x21, local copies, waits for them, and re-layouts  29.3 us
    dot_general x1, matrix products, on_device(): folded = jnp.dot(sensor_factor.T, residual, precision=highest)  27.7 us
    dot_general x1, matrix products, on_device(): jnp.dot(sensor_factor, flat_core, precision=highest)  26.3 us
    dot_general x1, matrix products, on_device(): jnp.dot(residual, flat_core.T, precision=highest)  20.9 us
  transfers between devices with their start and end apart: 3, of which 0 were waited for; matrix products, arithmetic and copies ran while one was open for 16% of the time, Pallas kernels for 0%

profile of v1, /device:TPU:0, one launch (start us, length us, event | category | flops | bytes accessed | tf_op | source)
XLA Modules:
  0.0 349.8 jit_solution(13775507985205720048)
XLA Ops:
  8.0 0.0 copy-start
  8.0 0.0 copy-start.6
  8.0 0.0 reduce-scatter.4.cloned.1.call-start
  8.1 24.9 %copy.27 = f32[768,64,128]{0,2,1:T(8,128)} copy(f32[768,64,128]{2,1,0:T(8,128)} %param.7) | data formatting | bytes 50331648 | tf_op args[0]
  32.9 0.0 copy-done
  32.9 0.0 copy-done.6
  32.9 0.0 copy-start.5
  33.0 1.8 fusion.32
  34.8 0.0 copy-done.5
  34.8 0.0 copy-start.1
  34.8 0.0 copy-start.3
  34.8 1.8 fusion.5
  36.7 0.0 copy-done.1
  36.7 0.0 copy-done.3
  36.7 26.3 %bitcast_subtract_fusion = f32[768,8192]{0,1:T(8,128)} fusion(f32[768,64,128]{0,2,1:T(8,128)} %copy.27, f32[768,64]{0,1:T(8,128)S(1)} %copy-done.3, f32[8,8,64,128]{3,2,1,0:T(8,128)S(1)} %bitcast.77), kind=kOutput, calls=%fused_computation.1 | convolution fusion | flops 4838129664 | bytes 52625408 | tf_op jit(solution)/shard_map/dot_general | solution.py:32
  63.0 0.0 copy-start.4
  63.0 20.9 %fusion.14 = f32[768,64]{0,1:T(8,128)S(1)} fusion(f32[768,8192]{0,1:T(8,128)} %bitcast_subtract_fusion, f32[8,8,64,128]{3,2,1,0:T(8,128)S(1)} %bitcast.78), kind=kOutput, calls=%fused_computation.18 | convolution fusion | flops 4831887360 | bytes 27459584 | tf_op jit(solution)/shard_map/dot_general | solution.py:36
  83.8 0.9 copy.34
  84.8 0.0 reduce-scatter.4.cloned.1.call-update
  84.8 0.0 all-gather.2.cloned.1.call-start
  84.8 0.5 all-gather.2.cloned.1.call-update
  85.4 0.0 all-reduce.2.cloned.1.call-start
  85.4 0.0 copy-done.4
  85.4 27.7 %convolution_bitcast_fusion = f32[8,8,64,128]{3,1,2,0:T(8,128)S(1)} fusion(f32[768,8192]{0,1:T(8,128)} %bitcast_subtract_fusion, f32[768,64]{0,1:T(8,128)S(1)} %copy-done.4), kind=kOutput, calls=%fused_computation.12 | convolution fusion | flops 4831838208 | bytes 27459584 | tf_op jit(solution)/shard_map/dot_general | solution.py:35
  113.1 0.4 copy.39
  113.5 1.9 fusion.28
  115.4 2.2 convolution_multiply_fusion
  117.6 0.0 all-reduce.2.cloned.1.call-update
  117.6 5.2 %fusion.20 = f32[128,64]{0,1:T(8,128)S(1)} fusion(f32[64,64,128]{2,1,0:T(8,128)S(1)} %bitcast.75, f32[64,64,64]{2,0,1:T(8,128)} %copy-done.1), kind=kOutput, calls=%fused_computation.20 | convolution fusion | flops 402661376 | bytes 3178496 | tf_op jit(solution)/shard_map/rkj,rks->js/dot_general | solution.py:44
  122.8 0.0 copy-start.7
  122.9 2.0 fusion.26
  124.8 0.0 copy-done.7
  124.8 0.1 copy.28
  124.9 0.1 reshape.31
  125.0 1.6 convert_reduce_fusion
  126.6 129.7 %psum.29 = f32[128,64]{0,1:T(8,128)} all-reduce(f32[128,64]{0,1:T(8,128)S(1)} %fusion.20), channel_id=1, replica_groups=mesh['sensor'=16,'channel'=4,'tm'=2] {'sensor','tm'}, use_global_device_ids=true, to_apply=%region_3.0 | all-reduce | flops 8192 | bytes 65536 | tf_op jit(solution)/shard_map/psum | solution.py:65
  256.3 3.0 fusion.23
  259.3 16.9 %psum.30 = f32[64,32]{0,1:T(8,128)S(1)} all-reduce(f32[64,32]{0,1:T(8,128)S(1)} %fusion.23), channel_id=1, replica_groups=mesh['sensor'=16,'channel'=4,'tm'=2] {'channel'}, use_global_device_ids=true, to_apply=%region_4.0 | all-reduce | flops 2048 | bytes 16384 | tf_op jit(solution)/shard_map/psum | solution.py:68
  276.2 52.9 %psum.31 = f32[64,32]{0,1:T(8,128)} all-reduce(f32[64,32]{0,1:T(8,128)S(1)} %psum.30), channel_id=1, replica_groups=mesh['sensor'=16,'channel'=4,'tm'=2] {'sensor'}, use_global_device_ids=true, to_apply=%region_5.0 | all-reduce | flops 2048 | bytes 16384 | tf_op jit(solution)/shard_map/psum | solution.py:68
  329.1 0.1 dynamic-slice
  329.2 0.0 reduce-scatter.4.cloned.1.call-done
  329.2 0.9 copy.35
  330.1 0.0 all-gather.2.cloned.1.call-done
  330.1 4.0 %copy_bitcast_fusion = f32[96,128,64]{1,2,0:T(8,128)} fusion(f32[12288,64]{0,1:T(8,128)} %all-gather.2.cloned.1.call-done), kind=kLoop, calls=%fused_computation.2 | loop fusion | bytes 6291456 | tf_op jit(solution)/shard_map/reshape | solution.py:12
  334.1 0.0 copy-start.2
  334.1 2.6 gather_fusion
  336.7 0.0 copy-done.2
  336.7 1.8 fusion.11
  338.5 1.6 fusion.25
  340.1 0.0 all-reduce.2.cloned.1.call-done
  340.1 2.3 copy.54
  (3 shorter events, 0.0 us)
Async XLA Ops:
  8.0 24.9 %copy-start = (f32[64,64,32]{1,2,0:T(8,128)S(1)}, f32[64,64,32]{1,2,0:T(8,128)}, u32[]{:S(2)}) copy-start(f32[64,64,32]{1,2,0:T(8,128)} %param.8) | copy-start | bytes 1572868
  8.0 24.9 %copy-start.6 = (f32[64,32]{0,1:T(8,128)S(1)}, f32[64,32]{0,1:T(8,128)}, u32[]{:S(2)}) copy-start(f32[64,32]{0,1:T(8,128)} %param.11) | copy-start | bytes 24580
  8.0 321.2 %reduce-scatter.4.cloned.1.call-start = ((), (), s32[]{:S(2)}) async-start(), calls=%async_computation.3 | async-start | bytes 442368
  32.9 1.9 copy-start.5
  34.8 1.9 copy-start.1
  34.8 1.9 copy-start.3
  63.0 22.5 %copy-start.4 = (f32[768,64]{0,1:T(8,128)S(1)}, f32[768,64]{0,1:T(8,128)}, u32[]{:S(2)}) copy-start(f32[768,64]{0,1:T(8,128)} %param.9) | copy-start | bytes 589828
  84.8 245.3 %all-gather.2.cloned.1.call-start = ((), (), s32[]{:S(2)}) async-start(), calls=%async_computation.2 | async-start | bytes 3342336 | tf_op jit(solution)/shard_map/all_gather | solution.py:57
  85.4 254.7 %all-reduce.2.cloned.1.call-start = ((), (), s32[]{:S(2)}) async-start(), calls=%async_computation.1 | async-start | bytes 2097152 | tf_op jit(solution)/shard_map/psum | solution.py:64
  122.8 2.0 copy-start.7
  334.1 2.6 copy-start.2
Sparse Core Ops, SparseCore 0:
  84.9 73.8 reduce-scatter.3
  164.1 146.0 all-reduce.1
Sparse Core Ops, SparseCore 1:
  87.0 38.2 all-gather.1
